TPU v7x, 256 devices: a whole 4x4x8 slice. The times are simulated.
256 devices in a mesh: lev: 64 (over z, x, core), col: 4 (over y).
Axes of the slice: x: 4, y: 4, z: 8, core: 2. Of those that a mesh axis runs over, the one named last changes fastest.
Arguments:
- probe_field: bfloat16 [128, 16, 4, 16384], P('lev', None, 'col'), may hold values from -6 to 6
- vertical_corr: bfloat16 [128, 128], replicated, may hold values from -0.5 to 0.5
- kernel_tiles: bfloat16 [4, 128, 9, 128, 128], P('col', 'lev'), may hold values from -0.1875 to 0.1875
- column_tile: int32 [4, 128, 9], P('col', 'lev'), may hold values from 0 to 511, as said below
- tile_counts: int32 [4, 128], P('col', 'lev'), may hold values from 1 to 9, as said below
Outputs:
- sketch: bfloat16 [128, 16, 4, 16384], P('lev', None, 'col')
Inputs may be any that keep to these rules, and one draw needn't show every extreme that they name: For k < tile_counts[j, q], column_tile[j, q, k] is the tile of band j + a at position (q + b) modulo 128, with a and b in -1, 0, 1 and band j + a within the bands; the used entries of one row tile are distinct, entry 0 is the row tile itself (j * 128 + q), and unused slots hold the row tile itself. `tile_counts`: row tiles of bands 1 and 2 use all 9 slots.
All inputs are finite; a program needn't handle non-finite values.
Results may differ from a plain program's by a relative error of at most 0.0049.
Values may be sent and summed in bfloat16 or wider, within the bound.
A program may use at most 64 MiB of HBM per device.

v0:
```python
import jax
import jax.numpy as jnp
from jax import lax
from jax.sharding import PartitionSpec as P


def padded(cells, sides, width):
    for axis, dim in sides:
        count = lax.axis_size(axis)
        head = lax.slice_in_dim(cells, 0, width, axis=dim)
        tail = lax.slice_in_dim(cells, cells.shape[dim] - width, cells.shape[dim], axis=dim)
        cells = jnp.concatenate(
            [
                lax.ppermute(tail, axis, [(i, (i + 1) % count) for i in range(count)]),
                cells,
                lax.ppermute(head, axis, [((i + 1) % count, i) for i in range(count)]),
            ],
            axis=dim,
        )
    return cells


def body(probe_field, vertical_corr, kernel_tiles, column_tile, tile_counts):
    level_count = lax.axis_size("lev")
    level_index = lax.axis_index("lev")
    band_index = lax.axis_index("col")
    columns = lax.all_to_all(probe_field, "lev", split_axis=3, concat_axis=0, tiled=True)
    levels = columns.shape[0]
    probes = columns.shape[1]
    tile_size = kernel_tiles.shape[-1]
    per_device = kernel_tiles.shape[1]
    slot_count = kernel_tiles.shape[2]
    band_total = per_device * level_count
    blocks = columns.reshape(levels, probes, 1, per_device, tile_size)
    extended = padded(blocks, (("lev", 3), ("col", 2)), 1)
    extended = extended.reshape(levels * probes, 3, per_device + 2, tile_size)
    local_ids = jnp.arange(per_device, dtype=jnp.int32)
    positions = level_index * per_device + local_ids
    neighbor = column_tile[0]
    target_band = neighbor // band_total
    target_position = neighbor % band_total
    delta_band = target_band - band_index
    delta_position = (target_position - positions[:, None] + band_total) % band_total
    offset_step = jnp.where(delta_position == band_total - 1, -1, delta_position)
    shift_index = (delta_band + 1) * 3 + offset_step + 1
    live_mask = jnp.arange(slot_count, dtype=jnp.int32)[None, :] < tile_counts[0][:, None]
    shift_table = (
        shift_index[:, :, None] == jnp.arange(9, dtype=jnp.int32)[None, None, :]
    ) & live_mask[:, :, None]
    shift_weights = jnp.einsum(
        "tks,tkoi->stoi",
        shift_table.astype(jnp.bfloat16),
        kernel_tiles[0],
        preferred_element_type=jnp.float32,
    ).astype(jnp.bfloat16)
    total = jnp.zeros((levels * probes, per_device, tile_size), jnp.float32)
    for band_step in range(3):
        for position_step in range(3):
            window = extended[:, band_step, position_step : position_step + per_device, :]
            total = total + jnp.einsum(
                "rti,toi->rto",
                window,
                shift_weights[band_step * 3 + position_step],
                preferred_element_type=jnp.float32,
            )
    horizontal = total.astype(jnp.bfloat16).reshape(levels, probes * per_device * tile_size)
    result = jnp.dot(vertical_corr, horizontal, preferred_element_type=jnp.float32).astype(
        jnp.bfloat16
    )
    result = result.reshape(levels, probes, 1, per_device * tile_size)
    return lax.all_to_all(result, "lev", split_axis=0, concat_axis=3, tiled=True)


def solution(mesh):
    placed = (
        P("lev", None, "col", None),
        P(),
        P("col", "lev", None, None, None),
        P("col", "lev", None),
        P("col", "lev"),
    )
    return jax.shard_map(
        body, mesh=mesh, in_specs=placed, out_specs=P("lev", None, "col", None), check_vma=False
    )
```

profile of v0, /device:TPU:1, one launch (start us, length us, event | category | flops | bytes accessed | tf_op | source)
XLA Modules:
  0.0 217.8 jit_solution(2704877317972603389)
XLA Ops:
  0.0 16.1 %copy.46 = bf16[2,16,1,16384]{1,0,2,3:T(2,128)(2,1)} copy(bf16[2,16,1,16384]{3,1,2,0:T(8,128)(2,1)} %param.5) | data formatting | bytes 2097152 | tf_op args[0]
  16.1 23.3 %reshape.128 = bf16[64,2,4096]{2,1,0:T(2,128)(2,1)S(1)} reshape(bf16[16384,1,2,16]{3,2,1,0:T(2,128)(2,1)} %bitcast.113) | data formatting | bytes 2097152
  39.4 40.8 %all_to_all.33 = bf16[64,2,4096]{2,1,0:T(2,128)(2,1)S(1)} all-to-all(bf16[64,2,4096]{2,1,0:T(2,128)(2,1)S(1)} %reshape.128), channel_id=1, replica_groups=mesh['lev'=64,'col'=4] {'lev'}, dimensions={0} | all-to-all | bytes 2097152 | tf_op jit(solution)/shard_map/all_to_all | solution.py:27
  80.2 7.5 %reshape.129 = bf16[16384,1,2,16]{3,2,1,0:T(2,128)(2,1)} reshape(bf16[64,2,4096]{2,1,0:T(2,128)(2,1)S(1)} %all_to_all.33) | data formatting | bytes 2097152
  87.7 11.8 %copy.59 = bf16[2,16,1,64,256]{4,3,1,0,2:T(8,128)(2,1)S(1)} copy(bf16[2,16,1,64,256]{1,0,4,3,2:T(2,128)(2,1)} %bitcast.112) | data formatting | bytes 2097152 | tf_op jit(solution)/shard_map/all_to_all | solution.py:27
  99.5 0.6 copy.48
  100.4 1.5 fusion.33
  102.0 2.5 %collective-permute-start = (bf16[128,16,1,1,128]{4,1,3,2,0:T(8,128)(2,1)S(1)}, bf16[128,16,1,1,128]{4,1,3,2,0:T(8,128)(2,1)S(1)}, u32[]{:S(2)}, u32[]{:S(2)}) collective-permute-start(bf16[128,16,1,1,128]{4,1,3,2,0:T(8,128)(2,1)S(1)} %copy.49), channel_id=1, source_target_pairs={{0,4},{4,8},{8,12},{12,16},{16,20},{20,24},{24,28},{28,32},{32,36}... | collective-permute-start | bytes 1572872 | tf_op jit(solution)/shard_map/ppermute | solution.py:14
  104.7 6.0 %collective-permute-done = bf16[128,16,1,1,128]{4,1,3,2,0:T(8,128)(2,1)S(1)} collective-permute-done((bf16[128,16,1,1,128]{4,1,3,2,0:T(8,128)(2,1)S(1)}, bf16[128,16,1,1,128]{4,1,3,2,0:T(8,128)(2,1)S(1)}, u32[]{:S(2)}, u32[]{:S(2)}) %collective-permute-start) | collective-permute-done | bytes 524320 | tf_op jit(solution)/shard_map/ppermute | solution.py:14
  110.6 0.8 copy.51
  111.5 2.1 collective-permute-done.1
  113.6 0.8 copy.52
  114.4 4.8 %pad_maximum_fusion.1 = bf16[128,16,1,4,128]{4,3,1,0,2:T(4,128)(2,1)} fusion(bf16[128,16,1,1,128]{4,3,1,0,2:T(2,128)(2,1)S(1)} %copy.52, bf16[128,16,1,2,128]{4,3,1,0,2:T(2,128)(2,1)S(1)} %reshape.123, bf16[128,16,1,1,128]{4,3,1,0,2:T(2,128)(2,1)S(1)} %copy.51), kind=kLoop, calls=%fused_computation.12 | loop fusion | flops 6291456 | bytes 4194304 | tf_op jit(solution)/shard_map/concatenate | solution.py:12
  119.3 1.3 collective-permute-start.2
  120.6 1.4 collective-permute-start.3
  122.2 0.5 fusion.2
  122.7 0.9 fusion.32
  123.6 41.8 %collective-permute-done.2 = bf16[128,16,1,4,128]{4,3,1,0,2:T(4,128)(2,1)} collective-permute-done((bf16[128,16,1,4,128]{4,3,1,0,2:T(4,128)(2,1)}, bf16[128,16,1,4,128]{4,3,1,0,2:T(4,128)(2,1)}, u32[]{:S(2)}, u32[]{:S(2)}) %collective-permute-start.2) | collective-permute-done | bytes 2097184 | tf_op jit(solution)/shard_map/ppermute | solution.py:14
  165.4 7.3 %pad_maximum_fusion = bf16[128,16,3,4,128]{4,3,1,0,2:T(4,128)(2,1)S(1)} fusion(bf16[128,16,1,4,128]{4,3,1,0,2:T(4,128)(2,1)} %collective-permute-done.3, bf16[128,16,1,1,128]{4,3,1,0,2:T(2,128)(2,1)S(1)} %copy-done.3, bf16[128,16,1,2,128]{4,3,1,0,2:T(2,128)(2,1)S(1)} %reshape.123, bf16[128,16,1,1,128]{4,3,1,0,2:T(2,128)(2,1)S(1)} %copy.51, ...), kind=kLoop, calls=%fused_computation | loop fusion | flops 31457280 | bytes 12582912 | tf_op jit(solution)/shard_map/concatenate | solution.py:12
  172.7 1.1 copy.53
  174.2 0.4 convolution_add_fusion.7
  175.1 0.4 convolution_add_fusion.5
  176.0 0.4 convolution_add_fusion.3
  176.5 0.4 convolution_add_fusion.2
  176.9 0.4 convolution_add_fusion.1
  177.4 0.4 fusion.1
  177.8 0.8 copy.54
  178.6 0.8 reshape.125
  179.5 0.5 convolution_convert_fusion
  180.0 0.9 copy.55
  180.9 35.9 %all_to_all.34 = bf16[128,16,1,256]{3,1,2,0:T(8,128)(2,1)S(1)} all-to-all(bf16[128,16,1,256]{3,1,2,0:T(8,128)(2,1)S(1)} %copy.55), channel_id=1, replica_groups=mesh['lev'=64,'col'=4] {'lev'}, dimensions={0} | all-to-all | bytes 2097152 | tf_op jit(solution)/shard_map/all_to_all | solution.py:71
  216.8 1.0 copy.69
  (25 shorter events, 2.0 us)
Async XLA Ops:
  0.0 122.2 %copy-start = (bf16[1,2,9,128,128]{4,3,2,1,0:T(8,128)(2,1)S(1)}, bf16[1,2,9,128,128]{4,3,2,1,0:T(8,128)(2,1)}, u32[]{:S(2)}) copy-start(bf16[1,2,9,128,128]{4,3,2,1,0:T(8,128)(2,1)} %param.7) | copy-start | bytes 1769476
  102.0 8.6 %collective-permute-start = (bf16[128,16,1,1,128]{4,1,3,2,0:T(8,128)(2,1)S(1)}, bf16[128,16,1,1,128]{4,1,3,2,0:T(8,128)(2,1)S(1)}, u32[]{:S(2)}, u32[]{:S(2)}) collective-permute-start(bf16[128,16,1,1,128]{4,1,3,2,0:T(8,128)(2,1)S(1)} %copy.49), channel_id=1, source_target_pairs={{0,4},{4,8},{8,12},{12,16},{16,20},{20,24},{24,28},{28,32},{32,36}... | collective-permute-start | bytes 1572872 | tf_op jit(solution)/shard_map/ppermute | solution.py:14
  104.6 9.0 %collective-permute-start.1 = (bf16[128,16,1,1,128]{4,1,3,2,0:T(8,128)(2,1)S(1)}, bf16[128,16,1,1,128]{4,1,3,2,0:T(8,128)(2,1)S(1)}, u32[]{:S(2)}, u32[]{:S(2)}) collective-permute-start(bf16[128,16,1,1,128]{4,1,3,2,0:T(8,128)(2,1)S(1)} %copy.50), channel_id=1, source_target_pairs={{4,0},{8,4},{12,8},{16,12},{20,16},{24,20},{28,24},{32,28},{36,32}... | collective-permute-start | bytes 1572872 | tf_op jit(solution)/shard_map/ppermute | solution.py:16
  114.4 4.9 %copy-start.2 = (bf16[128,16,1,1,128]{4,3,1,0,2:T(2,128)(2,1)}, bf16[128,16,1,1,128]{4,3,1,0,2:T(2,128)(2,1)S(1)}, u32[]{:S(2)}) copy-start(bf16[128,16,1,1,128]{4,3,1,0,2:T(2,128)(2,1)S(1)} %copy.52) | copy-start | bytes 1572868
  114.4 7.6 %copy-start.6 = (s32[1,2]{1,0:T(1,128)S(1)}, s32[1,2]{1,0:T(1,128)}, u32[]{:S(2)}) copy-start(s32[1,2]{1,0:T(1,128)} %param.9) | copy-start | bytes 28
  114.4 7.7 %copy-start.5 = (s32[1,2,9]{2,1,0:T(2,128)S(1)}, s32[1,2,9]{2,1,0:T(2,128)}, u32[]{:S(2)}) copy-start(s32[1,2,9]{2,1,0:T(2,128)} %param.8) | copy-start | bytes 220
  119.3 46.1 %collective-permute-start.2 = (bf16[128,16,1,4,128]{4,3,1,0,2:T(4,128)(2,1)}, bf16[128,16,1,4,128]{4,3,1,0,2:T(4,128)(2,1)}, u32[]{:S(2)}, u32[]{:S(2)}) collective-permute-start(bf16[128,16,1,4,128]{4,3,1,0,2:T(4,128)(2,1)} %pad_maximum_fusion.1), channel_id=1, source_target_pairs={{0,1},{1,2},{2,3},{3,0},{4,5},{5,6},{6,7},{7,4},{8,9},{9,10},{10,1... | collective-permute-start | bytes 6291464 | tf_op jit(solution)/shard_map/ppermute | solution.py:14
  120.6 44.8 %collective-permute-start.3 = (bf16[128,16,1,4,128]{4,3,1,0,2:T(4,128)(2,1)}, bf16[128,16,1,4,128]{4,3,1,0,2:T(4,128)(2,1)}, u32[]{:S(2)}, u32[]{:S(2)}) collective-permute-start(bf16[128,16,1,4,128]{4,3,1,0,2:T(4,128)(2,1)} %pad_maximum_fusion.1), channel_id=1, source_target_pairs={{1,0},{2,1},{3,2},{0,3},{5,4},{6,5},{7,6},{4,7},{9,8},{10,9},{11,1... | collective-permute-start | bytes 6291464 | tf_op jit(solution)/shard_map/ppermute | solution.py:16
  122.2 43.2 %copy-start.3 = (bf16[128,16,1,1,128]{4,3,1,0,2:T(2,128)(2,1)S(1)}, bf16[128,16,1,1,128]{4,3,1,0,2:T(2,128)(2,1)}, u32[]{:S(2)}) copy-start(bf16[128,16,1,1,128]{4,3,1,0,2:T(2,128)(2,1)} %copy-done.2) | copy-start | bytes 1572868
  177.8 1.6 copy-start.4
  180.0 37.9 %copy-start.1 = (bf16[1,2,9,128,128]{4,3,2,1,0:T(8,128)(2,1)S(1)}, bf16[1,2,9,128,128]{4,3,2,1,0:T(8,128)(2,1)}, u32[]{:S(2)}) copy-start(bf16[1,2,9,128,128]{4,3,2,1,0:T(8,128)(2,1)} %param.7) | copy-start | bytes 1769476
where the time goes:
time: 220 us; the launch traced here: 218 us
  blocking collectives  76.7 us (35%)
  local copies, waits for them, and re-layouts  68.5 us (31%)
  waiting for transfers between devices  49.8 us (23%)
  other arithmetic  12.3 us (6%)
  starting transfers between devices  5.34 us (2%)
  matrix products  4.95 us (2%)
    ppermute x2, waiting for transfers between devices, padded(): lax.ppermute(tail, axis, [(i, (i + 1) % count) for i in range(count)])  47.7 us
    unnamed x17, local copies, waits for them, and re-layouts  46.9 us
    all_to_all x1, blocking collectives, body(): lax.all_to_all(probe_field, 'lev', split_axis=3, concat_axis=0, tiled=True)  40.8 us
    all_to_all x1, blocking collectives, body(): lax.all_to_all(result, 'lev', split_axis=0, concat_axis=3, tiled=True)  35.9 us
    all_to_all x2, local copies, waits for them, and re-layouts, body(): lax.all_to_all(probe_field, 'lev', split_axis=3, concat_axis=0, tiled=True)  12.4 us
    concatenate x2, other arithmetic, padded(): jnp.concatenate([lax.ppermute(tail, axis, [(i, (i + 1) % count) for i in...  12.1 us
  transfers between devices with their start and end apart: 4, of which 3 were waited for; matrix products, arithmetic and copies ran while one was open for 1% of the time, Pallas kernels for 0%

commit v1 on v0

v1 whole, which is shorter than its diff:
```python
import functools

import jax
import jax.numpy as jnp
from jax import lax
from jax.experimental import pallas as pl
from jax.experimental.pallas import tpu as pltpu
from jax.sharding import PartitionSpec as P

MESH = pl.DeviceIdType.MESH
NZ = 8
NE = 8
NL = NZ * NE
TS = 128
LAG_EDGE = 2
LAG_SUM = 3


def offset(k):
    odd = lax.rem(k, 2)
    return odd * lax.div(k + 1, 2) - (1 - odd) * lax.div(k, 2)


def kernel(
    x_ref, v_ref, tiles_ref, slot_ref, count_ref, out_ref,
    field, weights, weights_in, kron, tiles, vert,
    own, part_out, part_in, mixed, result,
    sync, local_sem, x_send, x_recv, w_send, w_recv,
    e_send, e_recv, p_send, p_recv, b_send, b_recv,
):
    me = lax.axis_index("lev")
    band = lax.axis_index("col")
    z = lax.div(me, NE)
    e = lax.rem(me, NE)
    up = lax.rem(band + 1, 4)
    down = lax.rem(band + 3, 4)
    right = lax.rem(me + 1, NL)
    left = lax.rem(me + NL - 1, NL)

    tiles_copy = pltpu.make_async_copy(tiles_ref, tiles, local_sem.at[0])
    vert_copy = pltpu.make_async_copy(v_ref, vert, local_sem.at[1])
    tiles_copy.start()
    vert_copy.start()

    barrier = pltpu.get_barrier_semaphore()
    for i in range(1, NE):
        pl.semaphore_signal(
            barrier, inc=1, device_id={"lev": z * NE + lax.rem(e + i, NE)}, device_id_type=MESH
        )
    for i in range(1, NZ):
        pl.semaphore_signal(
            barrier, inc=1, device_id={"lev": lax.rem(z + i, NZ) * NE + e}, device_id_type=MESH
        )
    pl.semaphore_signal(barrier, inc=1, device_id={"col": up}, device_id_type=MESH)
    pl.semaphore_signal(barrier, inc=1, device_id={"col": down}, device_id_type=MESH)
    pl.semaphore_wait(barrier, NE + NZ)
    for i in range(1, NZ):
        pl.semaphore_signal(
            sync, inc=1, device_id={"lev": lax.rem(z + i, NZ) * NE + e}, device_id_type=MESH
        )
    pl.semaphore_wait(sync, NZ - 1)

    def columns(owner):
        return pl.ds(pl.multiple_of(owner * 256, 256), 256)

    def send_block(i, carry):
        there = lax.rem(z + offset(lax.div(i, NE)) + NZ, NZ)
        to = there * NE + lax.rem(e + lax.rem(i, NE), NE)
        pltpu.make_async_remote_copy(
            src_ref=x_ref.at[:, :, columns(to)],
            dst_ref=field.at[me, :, :, pl.ds(TS, 2 * TS)],
            send_sem=x_send,
            recv_sem=x_recv.at[z],
            device_id={"lev": to},
            device_id_type=MESH,
        ).start()
        return carry

    pltpu.make_async_copy(
        x_ref.at[:, :, columns(me)], field.at[me, :, :, pl.ds(TS, 2 * TS)], x_recv.at[z]
    ).start()
    lax.fori_loop(1, NL, send_block, 0)

    tiles_copy.wait()
    weights[...] = jnp.zeros_like(weights)
    for t in range(2):
        place = []
        for k in range(9):
            slot = slot_ref[t, k]
            step = lax.div(slot, 128) - band + 1
            shift = lax.rem(lax.rem(slot, 128) - (me * 2 + t) + 129 + 128, 128)
            live = count_ref[0, t] > k
            place.append(jnp.where(live, step * 3 + shift, -1))
        for a in range(3):
            for b in range(3):
                block = jnp.zeros((TS, TS), jnp.float32)
                for k in range(9):
                    hit = jnp.where(place[k] == a * 3 + b, 1.0, 0.0).astype(jnp.float32)
                    block = block + hit * tiles[t, k].astype(jnp.float32)
                weights[a, t * TS:(t + 1) * TS, (t + b) * TS:(t + b + 1) * TS] = block.astype(
                    jnp.bfloat16
                )
    w_up = pltpu.make_async_remote_copy(
        src_ref=weights.at[2], dst_ref=weights_in.at[0], send_sem=w_send.at[0],
        recv_sem=w_recv.at[0], device_id={"col": up}, device_id_type=MESH,
    )
    w_down = pltpu.make_async_remote_copy(
        src_ref=weights.at[0], dst_ref=weights_in.at[1], send_sem=w_send.at[1],
        recv_sem=w_recv.at[1], device_id={"col": down}, device_id_type=MESH,
    )
    w_up.start()
    w_down.start()

    vert_copy.wait()
    spread = (
        lax.div(lax.broadcasted_iota(jnp.int32, (TS, 1024), 1), 8)
        == lax.broadcasted_iota(jnp.int32, (TS, 1024), 0)
    ).astype(jnp.bfloat16)

    def kron_rows(c, carry):
        rows = (
            c * 16 + lax.div(lax.broadcasted_iota(jnp.int32, (TS, TS), 0), 8)
            == lax.broadcasted_iota(jnp.int32, (TS, TS), 1)
        ).astype(jnp.bfloat16)
        picked = jnp.dot(rows, vert[...], preferred_element_type=jnp.float32).astype(jnp.bfloat16)
        wide = jnp.dot(picked, spread, preferred_element_type=jnp.float32)
        same = lax.rem(lax.broadcasted_iota(jnp.int32, (TS, 1024), 0), 8) == lax.rem(
            lax.broadcasted_iota(jnp.int32, (TS, 1024), 1), 8
        )
        kron[pl.ds(pl.multiple_of(c * TS, TS), TS), :] = jnp.where(same, wide, 0.0).astype(
            jnp.bfloat16
        )
        return carry

    lax.fori_loop(0, 8, kron_rows, 0)

    w_up.wait()
    w_down.wait()

    def group(k):
        return lax.rem(z - offset(k) + NZ, NZ)

    def edge(g, side):
        source = field.at[pl.ds(g * NE, NE), :, :, pl.ds(TS if side == 0 else 2 * TS, TS)]
        target = field.at[pl.ds(g * NE, NE), :, :, pl.ds(3 * TS if side == 0 else 0, TS)]
        return pltpu.make_async_remote_copy(
            src_ref=source, dst_ref=target, send_sem=e_send.at[g, side],
            recv_sem=e_recv.at[g, side], device_id={"lev": left if side == 0 else right},
            device_id_type=MESH,
        )

    def part(g, side):
        return pltpu.make_async_remote_copy(
            src_ref=part_out.at[side, g], dst_ref=part_in.at[side, g],
            send_sem=p_send.at[g, side], recv_sem=p_recv.at[g, side],
            device_id={"col": down if side == 0 else up}, device_id_type=MESH,
        )

    nt = (((1,), (1,)), ((), ()))

    def step(k, carry):
        @pl.when(k < NZ)
        def _():
            g = group(k)
            arrived = field.at[pl.ds(g * NE, NE), :, :, pl.ds(TS, 2 * TS)]
            pltpu.make_async_copy(arrived, arrived, x_recv.at[g]).wait()
            edge(g, 0).start()
            edge(g, 1).start()

        @pl.when((k >= LAG_EDGE) & (k < NZ + LAG_EDGE))
        def _():
            g = group(k - LAG_EDGE)
            edge(g, 0).wait()
            edge(g, 1).wait()
            rows = field[pl.ds(g * NE, NE)].reshape(256, 4 * TS)
            for side in range(2):
                part_out[side, g] = lax.dot_general(
                    rows, weights_in[side], nt, preferred_element_type=jnp.float32
                ).astype(jnp.bfloat16)
                part(g, side).start()
            own[g] = lax.dot_general(rows, weights[1], nt, preferred_element_type=jnp.float32)

        @pl.when(k >= LAG_SUM)
        def _():
            g = group(k - LAG_SUM)
            part(g, 0).wait()
            part(g, 1).wait()
            total = own[g] + part_in[0, g].astype(jnp.float32) + part_in[1, g].astype(jnp.float32)
            total = total.reshape(16, 2, 8, 256)
            at = pl.ds(pl.multiple_of(g * TS, TS), TS)
            for half in range(2):
                mixed[half, at, :] = total[:, half].reshape(TS, 256).astype(jnp.bfloat16)

        return carry

    lax.fori_loop(0, NZ + LAG_SUM, step, 0)

    def answer(m, carry):
        there = lax.rem(z + offset(NZ - 1 - m) + NZ, NZ)
        rows = kron[pl.ds(pl.multiple_of(there * TS, TS), TS), :]
        halves = [
            jnp.dot(rows, mixed[half], preferred_element_type=jnp.float32).reshape(16, 1, 8, 256)
            for half in range(2)
        ]
        both = jnp.concatenate(halves, axis=1).reshape(NE, 2, 16, 256)
        result[pl.ds(there * NE, NE)] = both.astype(jnp.bfloat16)

        def send_back(i, inner):
            to = there * NE + lax.rem(e + i, NE)

            @pl.when(to != me)
            def _():
                pltpu.make_async_remote_copy(
                    src_ref=result.at[to], dst_ref=out_ref.at[:, :, columns(me)],
                    send_sem=b_send, recv_sem=b_recv, device_id={"lev": to}, device_id_type=MESH,
                ).start()

            @pl.when(to == me)
            def _():
                pltpu.make_async_copy(result.at[me], out_ref.at[:, :, columns(me)], b_recv).start()

            return inner

        lax.fori_loop(0, NE, send_back, 0)
        return carry

    lax.fori_loop(0, NZ, answer, 0)

    others = field.at[pl.ds(0, NL - 1), :, :, pl.ds(TS, 2 * TS)]
    pltpu.make_async_copy(others, others, x_send).wait()
    others = result.at[pl.ds(0, NL - 1)]
    pltpu.make_async_copy(others, others, b_send).wait()
    pltpu.make_async_copy(out_ref, out_ref, b_recv).wait()


def body(probe_field, vertical_corr, kernel_tiles, column_tile, tile_counts):
    bf16 = jnp.bfloat16
    dma = pltpu.SemaphoreType.DMA
    any_space = pl.BlockSpec(memory_space=pl.ANY)
    smem = pl.BlockSpec(memory_space=pltpu.SMEM)
    out = pl.pallas_call(
        kernel,
        out_shape=jax.ShapeDtypeStruct((2, 16, NL * 256), bf16),
        in_specs=[any_space, any_space, any_space, smem, smem],
        out_specs=any_space,
        scratch_shapes=[
            pltpu.VMEM((NL, 2, 16, 4 * TS), bf16),
            pltpu.VMEM((3, 256, 512), bf16),
            pltpu.VMEM((2, 256, 512), bf16),
            pltpu.VMEM((1024, 1024), bf16),
            pltpu.VMEM((2, 9, TS, TS), bf16),
            pltpu.VMEM((TS, TS), bf16),
            pltpu.VMEM((NZ, 256, 256), jnp.float32),
            pltpu.VMEM((2, NZ, 256, 256), bf16),
            pltpu.VMEM((2, NZ, 256, 256), bf16),
            pltpu.VMEM((2, 1024, 256), bf16),
            pltpu.VMEM((NL, 2, 16, 256), bf16),
            pltpu.SemaphoreType.REGULAR,
            dma((2,)),
            dma,
            dma((NZ,)),
            dma((2,)),
            dma((2,)),
            dma((NZ, 2)),
            dma((NZ, 2)),
            dma((NZ, 2)),
            dma((NZ, 2)),
            dma,
            dma,
        ],
        compiler_params=pltpu.CompilerParams(
            collective_id=0, has_side_effects=True, vmem_limit_bytes=40 * 1024 * 1024
        ),
    )(
        probe_field.reshape(2, 16, NL * 256),
        vertical_corr,
        kernel_tiles.reshape(2, 9, TS, TS),
        column_tile.reshape(2, 9),
        tile_counts,
    )
    return out.reshape(2, 16, 1, NL * 256)


def solution(mesh):
    placed = (
        P("lev", None, "col", None),
        P(),
        P("col", "lev", None, None, None),
        P("col", "lev", None),
        P("col", "lev"),
    )
    return jax.shard_map(
        body, mesh=mesh, in_specs=placed, out_specs=P("lev", None, "col", None), check_vma=False
    )
```

time: 220 us -> 99.5 us (0.45)
  Pallas kernels: 0 us -> 94.5 us
  blocking collectives: 76.7 us -> 0 us
  local copies, waits for them, and re-layouts: 68.5 us -> 4.7 us
  waiting for transfers between devices: 49.8 us -> 0 us
  other arithmetic: 12.3 us -> 0 us
  starting transfers between devices: 5.34 us -> 0 us
  matrix products: 4.95 us -> 0 us
    pallas_call x0 -> x1, Pallas kernels: none -> 94.5 us  [body(): pl.pallas_call(kernel, out_shape=jax.ShapeDtypeStruct((2, 16, NL * 256),...]
    all_to_all x2 -> x0, blocking collectives: 76.7 us -> none  [the longest x1 40.8 us: body(): lax.all_to_all(probe_field, 'lev', split_axis=3, concat_axis=0, tiled=True)]
    ppermute x4 -> x0, waiting for transfers between devices: 49.8 us -> none  [the longest x2 47.7 us: padded(): lax.ppermute(tail, axis, [(i, (i + 1) % count) for i in range(count)])]
    unnamed x17 -> x11, local copies, waits for them, and re-layouts: 46.9 us -> 4.7 us
    all_to_all x3 -> x0, local copies, waits for them, and re-layouts: 13.5 us -> none  [the longest x2 12.4 us: body(): lax.all_to_all(probe_field, 'lev', split_axis=3, concat_axis=0, tiled=True)]
    concatenate x2 -> x0, other arithmetic: 12.1 us -> none  [padded(): jnp.concatenate([lax.ppermute(tail, axis, [(i, (i + 1) % count) for i in...]
    ppermute x4 -> x0, starting transfers between devices: 5.34 us -> none  [the longest x2 3.81 us: padded(): lax.ppermute(tail, axis, [(i, (i + 1) % count) for i in range(count)])]
    dot_general x11 -> x0, matrix products: 4.95 us -> none  [the longest x9 3.97 us: body(): jnp.einsum('rti,toi->rto', window, shift_weights[band_step * 3 + position...]
  transfers between devices with their start and end apart: 4 -> 0, of which waited for: 3 -> 0; matrix products, arithmetic and copies ran while one was open for 1% -> 0% of each run, Pallas kernels for 0% -> 0%
where the time goes in v1:
time: 99.5 us; the launch traced here: 99.3 us
  Pallas kernels  94.5 us (95%)
  local copies, waits for them, and re-layouts  4.7 us (5%)
    pallas_call x1, Pallas kernels, body(): pl.pallas_call(kernel, out_shape=jax.ShapeDtypeStruct((2, 16, NL * 256),...  94.5 us
    unnamed x11, local copies, waits for them, and re-layouts  4.7 us

profile of v1, /device:TPU:1, one launch (start us, length us, event | category | flops | bytes accessed | tf_op | source)
XLA Modules:
  0.0 99.3 jit_solution(5820905388304739160)
XLA Ops:
  0.0 0.0 copy-start.3
  0.0 0.0 copy-start.4
  0.0 0.7 copy-done.3
  0.7 0.0 copy-done.4
  0.7 0.0 copy-start
  0.7 1.2 %copy-done = bf16[2,16,1,16384]{3,1,2,0:T(8,128)(2,1)S(1)} copy-done((bf16[2,16,1,16384]{3,1,2,0:T(8,128)(2,1)S(1)}, bf16[2,16,1,16384]{3,1,2,0:T(8,128)(2,1)}, u32[]{:S(2)}) %copy-start) | copy-done | bytes 1048600
  1.9 0.0 copy-start.1
  1.9 1.1 %copy-done.1 = bf16[1,2,9,128,128]{4,3,2,1,0:T(8,128)(2,1)S(1)} copy-done((bf16[1,2,9,128,128]{4,3,2,1,0:T(8,128)(2,1)S(1)}, bf16[1,2,9,128,128]{4,3,2,1,0:T(8,128)(2,1)}, u32[]{:S(2)}) %copy-start.1) | copy-done | bytes 589848
  3.0 0.0 copy-start.2
  3.0 0.8 copy-done.2
  3.7 94.5 %shard_map.55 = bf16[2,16,16384]{2,1,0:T(8,128)(2,1)S(1)} custom-call(bf16[2,16,16384]{2,1,0:T(8,128)(2,1)S(1)} %bitcast.7, bf16[128,128]{1,0:T(8,128)(2,1)S(1)} %copy-done.2, bf16[2,9,128,128]{3,2,1,0:T(8,128)(2,1)S(1)} %bitcast.8, s32[2,9]{1,0:T(2,128)S(1)} %bitcast.9, s32[1,2]{1,0:T(1,128)S(1)} %copy-done.4), custom_call_target="tpu_custom_call" | custom-call | tf_op jit(solution)/shard_map/pallas_call | solution.py:241
  98.3 1.0 copy.8
Async XLA Ops:
  0.0 0.7 copy-start.3
  0.0 0.7 copy-start.4
  0.7 1.2 %copy-start = (bf16[2,16,1,16384]{3,1,2,0:T(8,128)(2,1)S(1)}, bf16[2,16,1,16384]{3,1,2,0:T(8,128)(2,1)}, u32[]{:S(2)}) copy-start(bf16[2,16,1,16384]{3,1,2,0:T(8,128)(2,1)} %param.5) | copy-start | bytes 3145732
  1.9 1.1 %copy-start.1 = (bf16[1,2,9,128,128]{4,3,2,1,0:T(8,128)(2,1)S(1)}, bf16[1,2,9,128,128]{4,3,2,1,0:T(8,128)(2,1)}, u32[]{:S(2)}) copy-start(bf16[1,2,9,128,128]{4,3,2,1,0:T(8,128)(2,1)} %param.7) | copy-start | bytes 1769476
  3.0 0.8 copy-start.2

commit v2 on v1

v2 whole, which is shorter than its diff:
```python
import jax
import jax.numpy as jnp
from jax import lax
from jax.experimental import pallas as pl
from jax.experimental.pallas import tpu as pltpu
from jax.sharding import PartitionSpec as P

MESH = pl.DeviceIdType.MESH
NZ = 8
NX = 4
NE = 2 * NX
NL = NZ * NE
TS = 128
ROUNDS = 2 * NX
WINDOW = 3
LAG_EDGE = 2
LAG_SUM = 3


def offset(k):
    odd = lax.rem(k, 2)
    return odd * lax.div(k + 1, 2) - (1 - odd) * lax.div(k, 2)


def kernel(
    x_ref, v_ref, tiles_ref, slot_hbm, count_hbm, out_ref,
    field, weights, weights_in, kron, tiles, vert, slot_ref, count_ref,
    own, part_out, part_in, mixed, result,
    local_sem, x_send, x_recv, w_send, w_recv,
    e_send, e_recv, p_send, p_recv, b_send, b_recv,
):
    me = lax.axis_index("lev")
    band = lax.axis_index("col")
    z = lax.div(me, NE)
    e = lax.rem(me, NE)
    x = lax.div(e, 2)
    core = lax.rem(e, 2)
    up = lax.rem(band + 1, 4)
    down = lax.rem(band + 3, 4)
    right = lax.rem(me + 1, NL)
    left = lax.rem(me + NL - 1, NL)

    barrier = pltpu.get_barrier_semaphore()

    def greet(i, carry):
        pl.semaphore_signal(
            barrier, inc=1, device_id={"lev": lax.rem(me + i, NL)}, device_id_type=MESH
        )
        return carry

    pl.semaphore_signal(barrier, inc=1, device_id={"col": up}, device_id_type=MESH)
    pl.semaphore_signal(barrier, inc=1, device_id={"col": down}, device_id_type=MESH)
    lax.fori_loop(1, NL, greet, 0)

    local = [
        pltpu.make_async_copy(source, target, local_sem.at[i])
        for i, (source, target) in enumerate(
            [(slot_hbm, slot_ref), (count_hbm, count_ref), (tiles_ref, tiles), (v_ref, vert)]
        )
    ]
    for copy in local:
        copy.start()

    pl.semaphore_wait(barrier, NL + 1)

    def columns(owner):
        return pl.ds(pl.multiple_of(owner * 256, 256), 256)

    def send_block(k, i):
        half = lax.div(k, NX)
        there = lax.rem(z + offset(lax.div(i, 2)) + NZ, NZ)
        place = lax.rem(x + lax.rem(k, NX), NX) * 2 + lax.rem(core + lax.rem(i, 2), 2)
        to = there * NE + place
        pltpu.make_async_remote_copy(
            src_ref=x_ref.at[:, half, :, columns(to)],
            dst_ref=field.at[half, z, e, :, :, pl.ds(TS, 2 * TS)],
            send_sem=x_send.at[k],
            recv_sem=x_recv.at[half, x],
            device_id={"lev": to},
            device_id_type=MESH,
        ).start()

    def keep_block(half):
        pltpu.make_async_copy(
            x_ref.at[:, half, :, columns(me)],
            field.at[half, z, e, :, :, pl.ds(TS, 2 * TS)],
            x_recv.at[half, x],
        ).start()

    def send_round(k, first=0):
        def one(i, carry):
            send_block(k, i)
            return carry

        lax.fori_loop(first, 2 * NZ, one, 0)

    send_round(0, 1)
    keep_block(0)
    keep_block(1)
    for k in range(1, WINDOW):
        send_round(k)

    for copy in local[:3]:
        copy.wait()
    nothing = jnp.zeros((TS, TS), jnp.bfloat16)
    for t in range(2):
        unused = pl.ds((1 - t) * 3 * TS, TS)
        for side in range(2):
            weights_in[side, t * TS:(t + 1) * TS, unused] = nothing
        weights[1, t * TS:(t + 1) * TS, unused] = nothing
        place = []
        for k in range(9):
            slot = slot_ref[t, k]
            step = lax.div(slot, 128) - band + 1
            shift = lax.rem(lax.rem(slot, 128) - (me * 2 + t) + 129 + 128, 128)
            live = count_ref[0, t] > k
            place.append(jnp.where(live, step * 3 + shift, -1))
        for a in range(3):
            for b in range(3):
                block = jnp.zeros((TS, TS), jnp.float32)
                for k in range(9):
                    hit = jnp.where(place[k] == a * 3 + b, 1.0, 0.0).astype(jnp.float32)
                    block = block + hit * tiles[t, k].astype(jnp.float32)
                weights[a, t * TS:(t + 1) * TS, (t + b) * TS:(t + b + 1) * TS] = block.astype(
                    jnp.bfloat16
                )
    matrices = []
    for side in range(2):
        for t in range(2):
            at = (pl.ds(t * TS, TS), pl.ds(t * TS, 3 * TS))
            matrices.append(
                pltpu.make_async_remote_copy(
                    src_ref=weights.at[(2 - 2 * side, *at)],
                    dst_ref=weights_in.at[(side, *at)],
                    send_sem=w_send.at[side, t],
                    recv_sem=w_recv.at[side, t],
                    device_id={"col": down if side else up},
                    device_id_type=MESH,
                )
            )
    for copy in matrices:
        copy.start()

    local[3].wait()
    spread = (
        lax.div(lax.broadcasted_iota(jnp.int32, (TS, 1024), 1), 8)
        == lax.broadcasted_iota(jnp.int32, (TS, 1024), 0)
    ).astype(jnp.bfloat16)

    def kron_rows(c, carry):
        rows = (
            c * 16 + lax.div(lax.broadcasted_iota(jnp.int32, (TS, TS), 0), 8)
            == lax.broadcasted_iota(jnp.int32, (TS, TS), 1)
        ).astype(jnp.bfloat16)
        picked = jnp.dot(rows, vert[...], preferred_element_type=jnp.float32).astype(jnp.bfloat16)
        wide = jnp.dot(picked, spread, preferred_element_type=jnp.float32)
        same = lax.rem(lax.broadcasted_iota(jnp.int32, (TS, 1024), 0), 8) == lax.rem(
            lax.broadcasted_iota(jnp.int32, (TS, 1024), 1), 8
        )
        kron[c] = jnp.where(same, wide, 0.0).reshape(NX, 32, 1024).astype(jnp.bfloat16)
        return carry

    lax.fori_loop(0, 8, kron_rows, 0)

    def group(r):
        return lax.rem(x - r + NX, NX)

    def edge(half, g, side):
        rows = (half, slice(None), pl.ds(g * 2, 2), slice(None), slice(None))
        return pltpu.make_async_remote_copy(
            src_ref=field.at[(*rows, pl.ds(TS if side == 0 else 2 * TS, TS))],
            dst_ref=field.at[(*rows, pl.ds(3 * TS if side == 0 else 0, TS))],
            send_sem=e_send.at[half, g, side],
            recv_sem=e_recv.at[half, g, side],
            device_id={"lev": left if side == 0 else right},
            device_id_type=MESH,
        )

    def part(half, g, side):
        return pltpu.make_async_remote_copy(
            src_ref=part_out.at[side, half, g],
            dst_ref=part_in.at[side, half, g],
            send_sem=p_send.at[half, g, side],
            recv_sem=p_recv.at[half, g, side],
            device_id={"col": down if side == 0 else up},
            device_id_type=MESH,
        )

    nt = (((1,), (1,)), ((), ()))

    def answer(half):
        def one_round(r, carry):
            place = lax.rem(x + r, NX)
            rows = kron[:, place].reshape(256, 1024)
            block = jnp.dot(
                rows, mixed[half].reshape(1024, 256), preferred_element_type=jnp.float32
            )
            result[half, :, pl.ds(place * 2, 2)] = block.reshape(NZ, 2, 2, 8, 256).astype(
                jnp.bfloat16
            )

            def send_back(i, inner):
                there = lax.rem(z + offset(lax.div(i, 2)) + NZ, NZ)
                spot = place * 2 + lax.rem(core + lax.rem(i, 2), 2)
                to = there * NE + spot

                @pl.when(to != me)
                def _():
                    pltpu.make_async_remote_copy(
                        src_ref=result.at[half, there, spot],
                        dst_ref=out_ref.at[:, half, :, columns(me)],
                        send_sem=b_send,
                        recv_sem=b_recv,
                        device_id={"lev": to},
                        device_id_type=MESH,
                    ).start()

                @pl.when(to == me)
                def _():
                    pltpu.make_async_copy(
                        result.at[half, z, e], out_ref.at[:, half, :, columns(me)], b_recv
                    ).start()

                return inner

            lax.fori_loop(0, 2 * NZ, send_back, 0)
            return carry

        lax.fori_loop(0, NX, one_round, 0)

    def step(k, carry):
        @pl.when(k < ROUNDS)
        def _():
            half = lax.div(k, NX)
            g = group(lax.rem(k, NX))
            arrived = field.at[half, :, pl.ds(g * 2, 2), :, :, pl.ds(TS, 2 * TS)]
            pltpu.make_async_copy(arrived, arrived, x_recv.at[half, g]).wait()
            edge(half, g, 0).start()
            edge(half, g, 1).start()

        @pl.when(k < ROUNDS - WINDOW)
        def _():
            later = k + WINDOW
            send_round(later, jnp.where(later == NX, 1, 0))

        @pl.when(k == LAG_EDGE)
        def _():
            for copy in matrices:
                copy.wait()

        @pl.when((k >= LAG_EDGE) & (k < ROUNDS + LAG_EDGE))
        def _():
            now = k - LAG_EDGE
            half = lax.div(now, NX)
            g = group(lax.rem(now + 1, NX))
            edge(half, g, 0).wait()
            edge(half, g, 1).wait()
            rows = field[half, :, pl.ds(g * 2, 2)].reshape(256, 4 * TS)
            for side in range(2):
                part_out[side, half, g] = lax.dot_general(
                    rows, weights_in[side], nt, preferred_element_type=jnp.float32
                ).astype(jnp.bfloat16)
                part(half, g, side).start()
            own[half, g] = lax.dot_general(
                rows, weights[1], nt, preferred_element_type=jnp.float32
            )

        @pl.when(k >= LAG_SUM)
        def _():
            now = k - LAG_SUM
            half = lax.div(now, NX)
            g = group(lax.rem(now + 1, NX))
            part(half, g, 0).wait()
            part(half, g, 1).wait()
            total = (
                own[half, g]
                + part_in[0, half, g].astype(jnp.float32)
                + part_in[1, half, g].astype(jnp.float32)
            )
            mixed[half, :, g] = total.reshape(NZ, 32, 256).astype(jnp.bfloat16)

            @pl.when(lax.rem(now, NX) == NX - 1)
            def _():
                answer(half)

        return carry

    lax.fori_loop(0, ROUNDS + LAG_SUM, step, 0)

    for k in range(ROUNDS):
        if k % NX == 0:
            for rows in ((pl.ds(0, NZ - 1), pl.ds(0, 2)), (NZ - 1, pl.ds(0, 1))):
                block = field.at[(0, *rows, slice(None), slice(None), pl.ds(TS, 2 * TS))]
                pltpu.make_async_copy(block, block, x_send.at[k]).wait()
        else:
            block = field.at[0, :, pl.ds(0, 2), :, :, pl.ds(TS, 2 * TS)]
            pltpu.make_async_copy(block, block, x_send.at[k]).wait()
    block = out_ref.at[:, :, :, pl.ds(0, (NL - 1) * 256)]
    pltpu.make_async_copy(block, block, b_send).wait()
    pltpu.make_async_copy(out_ref, out_ref, b_recv).wait()


def body(probe_field, vertical_corr, kernel_tiles, column_tile, tile_counts):
    bf16 = jnp.bfloat16
    dma = pltpu.SemaphoreType.DMA
    any_space = pl.BlockSpec(memory_space=pl.ANY)
    operands = [
        probe_field.reshape(2, 2, 8, NL * 256),
        vertical_corr,
        kernel_tiles.reshape(2, 9, TS, TS),
        column_tile.reshape(2, 9),
        tile_counts,
    ]
    operands = [pltpu.with_memory_space_constraint(a, pltpu.HBM) for a in operands]
    out = pl.pallas_call(
        kernel,
        out_shape=jax.ShapeDtypeStruct((2, 2, 8, NL * 256), bf16),
        in_specs=[any_space] * 5,
        out_specs=any_space,
        scratch_shapes=[
            pltpu.VMEM((2, NZ, NE, 2, 8, 4 * TS), bf16),
            pltpu.VMEM((3, 256, 512), bf16),
            pltpu.VMEM((2, 256, 512), bf16),
            pltpu.VMEM((NZ, NX, 32, 1024), bf16),
            pltpu.VMEM((2, 9, TS, TS), bf16),
            pltpu.VMEM((TS, TS), bf16),
            pltpu.SMEM((2, 9), jnp.int32),
            pltpu.SMEM((1, 2), jnp.int32),
            pltpu.VMEM((2, NX, 256, 256), jnp.float32),
            pltpu.VMEM((2, 2, NX, 256, 256), bf16),
            pltpu.VMEM((2, 2, NX, 256, 256), bf16),
            pltpu.VMEM((2, NZ, NX, 32, 256), bf16),
            pltpu.VMEM((2, NZ, NE, 2, 8, 256), bf16),
            dma((4,)),
            dma((ROUNDS,)),
            dma((2, NX)),
            dma((2, 2)),
            dma((2, 2)),
            dma((2, NX, 2)),
            dma((2, NX, 2)),
            dma((2, NX, 2)),
            dma((2, NX, 2)),
            dma,
            dma,
        ],
        compiler_params=pltpu.CompilerParams(
            collective_id=0, has_side_effects=True, vmem_limit_bytes=40 * 1024 * 1024
        ),
    )(*operands)
    return out.reshape(2, 16, 1, NL * 256)


def solution(mesh):
    placed = (
        P("lev", None, "col", None),
        P(),
        P("col", "lev", None, None, None),
        P("col", "lev", None),
        P("col", "lev"),
    )
    return jax.shard_map(
        body, mesh=mesh, in_specs=placed, out_specs=P("lev", None, "col", None), check_vma=False
    )
```

time: 99.5 us -> 78.2 us (0.79)
  Pallas kernels: 94.5 us -> 76.2 us
  local copies, waits for them, and re-layouts: 4.7 us -> 0.97 us
    pallas_call x1, Pallas kernels: 94.5 us -> 76.2 us  [body(): pl.pallas_call(kernel, out_shape=jax.ShapeDtypeStruct((2, 2, 8, NL * 256)...]
    unnamed x11 -> x1, local copies, waits for them, and re-layouts: 4.7 us -> 0.97 us
where the time goes in v2:
time: 78.2 us; the launch traced here: 77.2 us
  Pallas kernels  76.2 us (97%)
  local copies, waits for them, and re-layouts  0.97 us (1%)
    pallas_call x1, Pallas kernels, body(): pl.pallas_call(kernel, out_shape=jax.ShapeDtypeStruct((2, 2, 8, NL * 256)...  76.2 us

profile of v2, /device:TPU:1, one launch (start us, length us, event | category | flops | bytes accessed | tf_op | source)
XLA Modules:
  0.0 77.2 jit_solution(4035194807539000481)
XLA Ops:
  0.0 76.2 %shard_map.55 = bf16[2,2,8,16384]{3,2,1,0:T(8,128)(2,1)S(1)} custom-call(bf16[2,2,8,16384]{3,2,1,0:T(8,128)(2,1)} %bitcast.7, bf16[128,128]{1,0:T(8,128)(2,1)} %v_ref.1, bf16[2,9,128,128]{3,2,1,0:T(8,128)(2,1)} %bitcast.8, s32[2,9]{1,0:T(2,128)} %bitcast.9, s32[1,2]{1,0:T(1,128)} %count_hbm.1), custom_call_target="tpu_custom_call" | custom-call | tf_op jit(solution)/shard_map/pallas_call | solution.py:315
  76.2 1.0 %copy.8 = bf16[2,16,1,16384]{3,1,2,0:T(8,128)(2,1)} copy(bf16[2,16,1,16384]{3,1,2,0:T(8,128)(2,1)S(1)} %bitcast.6) | data formatting | bytes 2097152

commit v3 on v2

--- a/solution.py
+++ b/solution.py
@@ -14,7 +14,7 @@
 ROUNDS = 2 * NX
 WINDOW = 3
 LAG_EDGE = 2
-LAG_SUM = 3
+LAG_SUM = 4
 
 
 def offset(k):
@@ -60,45 +60,6 @@
     ]
     for copy in local:
         copy.start()
-
-    pl.semaphore_wait(barrier, NL + 1)
-
-    def columns(owner):
-        return pl.ds(pl.multiple_of(owner * 256, 256), 256)
-
-    def send_block(k, i):
-        half = lax.div(k, NX)
-        there = lax.rem(z + offset(lax.div(i, 2)) + NZ, NZ)
-        place = lax.rem(x + lax.rem(k, NX), NX) * 2 + lax.rem(core + lax.rem(i, 2), 2)
-        to = there * NE + place
-        pltpu.make_async_remote_copy(
-            src_ref=x_ref.at[:, half, :, columns(to)],
-            dst_ref=field.at[half, z, e, :, :, pl.ds(TS, 2 * TS)],
-            send_sem=x_send.at[k],
-            recv_sem=x_recv.at[half, x],
-            device_id={"lev": to},
-            device_id_type=MESH,
-        ).start()
-
-    def keep_block(half):
-        pltpu.make_async_copy(
-            x_ref.at[:, half, :, columns(me)],
-            field.at[half, z, e, :, :, pl.ds(TS, 2 * TS)],
-            x_recv.at[half, x],
-        ).start()
-
-    def send_round(k, first=0):
-        def one(i, carry):
-            send_block(k, i)
-            return carry
-
-        lax.fori_loop(first, 2 * NZ, one, 0)
-
-    send_round(0, 1)
-    keep_block(0)
-    keep_block(1)
-    for k in range(1, WINDOW):
-        send_round(k)
 
     for copy in local[:3]:
         copy.wait()
@@ -138,8 +99,48 @@
                     device_id_type=MESH,
                 )
             )
+
+    pl.semaphore_wait(barrier, NL + 1)
     for copy in matrices:
         copy.start()
+
+    def columns(owner):
+        return pl.ds(pl.multiple_of(owner * 256, 256), 256)
+
+    def send_block(k, i):
+        half = lax.div(k, NX)
+        there = lax.rem(z + offset(lax.div(i, 2)) + NZ, NZ)
+        place = lax.rem(x + lax.rem(k, NX), NX) * 2 + lax.rem(core + lax.rem(i, 2), 2)
+        to = there * NE + place
+        pltpu.make_async_remote_copy(
+            src_ref=x_ref.at[:, half, :, columns(to)],
+            dst_ref=field.at[half, z, e, :, :, pl.ds(TS, 2 * TS)],
+            send_sem=x_send.at[k],
+            recv_sem=x_recv.at[half, x],
+            device_id={"lev": to},
+            device_id_type=MESH,
+        ).start()
+
+    def keep_block(half):
+        pltpu.make_async_copy(
+            x_ref.at[:, half, :, columns(me)],
+            field.at[half, z, e, :, :, pl.ds(TS, 2 * TS)],
+            x_recv.at[half, x],
+        ).start()
+
+    def send_round(k, first=0):
+        def one(i, carry):
+            send_block(k, i)
+            return carry
+
+        lax.fori_loop(first, 2 * NZ, one, 0)
+
+    send_round(0, 1)
+    keep_block(0)
+    keep_block(1)
+    for k in range(1, WINDOW):
+        send_round(k)
+
 
     local[3].wait()
     spread = (

time: 78.2 us -> 73.8 us (0.944); the launches traced: 77.2 us -> 73.7 us
  Pallas kernels: 76.2 us -> 72.7 us
    pallas_call x1, Pallas kernels: 76.2 us -> 72.7 us  [body(): pl.pallas_call(kernel, out_shape=jax.ShapeDtypeStruct((2, 2, 8, NL * 256)...]
where the time goes in v3:
time: 73.8 us; the launch traced here: 73.7 us
  Pallas kernels  72.7 us (99%)
  local copies, waits for them, and re-layouts  0.97 us (1%)
    pallas_call x1, Pallas kernels, body(): pl.pallas_call(kernel, out_shape=jax.ShapeDtypeStruct((2, 2, 8, NL * 256)...  72.7 us

profile of v3, /device:TPU:1, one launch (start us, length us, event | category | flops | bytes accessed | tf_op | source)
XLA Modules:
  0.0 73.7 jit_solution(14649758926933756132)
XLA Ops:
  0.0 72.7 %shard_map.55 = bf16[2,2,8,16384]{3,2,1,0:T(8,128)(2,1)S(1)} custom-call(bf16[2,2,8,16384]{3,2,1,0:T(8,128)(2,1)} %bitcast.7, bf16[128,128]{1,0:T(8,128)(2,1)} %v_ref.1, bf16[2,9,128,128]{3,2,1,0:T(8,128)(2,1)} %bitcast.8, s32[2,9]{1,0:T(2,128)} %bitcast.9, s32[1,2]{1,0:T(1,128)} %count_hbm.1), custom_call_target="tpu_custom_call" | custom-call | tf_op jit(solution)/shard_map/pallas_call | solution.py:316
  72.7 1.0 %copy.8 = bf16[2,16,1,16384]{3,1,2,0:T(8,128)(2,1)} copy(bf16[2,16,1,16384]{3,1,2,0:T(8,128)(2,1)S(1)} %bitcast.6) | data formatting | bytes 2097152

commit v4 on v3

--- a/solution.py
+++ b/solution.py
@@ -11,15 +11,14 @@
 NE = 2 * NX
 NL = NZ * NE
 TS = 128
+ENDS = (NE - 1, 0)
 ROUNDS = 2 * NX
 WINDOW = 3
 LAG_EDGE = 2
 LAG_SUM = 4
 
 
-def offset(k):
-    odd = lax.rem(k, 2)
-    return odd * lax.div(k + 1, 2) - (1 - odd) * lax.div(k, 2)
+OFFSETS = (0, 1, -1, 2, -2, 3, -3, 4)
 
 
 def kernel(
@@ -27,7 +26,7 @@
     field, weights, weights_in, kron, tiles, vert, slot_ref, count_ref,
     own, part_out, part_in, mixed, result,
     local_sem, x_send, x_recv, w_send, w_recv,
-    e_send, e_recv, p_send, p_recv, b_send, b_recv,
+    t_send, e_send, e_recv, p_send, p_recv, b_send, b_recv,
 ):
     me = lax.axis_index("lev")
     band = lax.axis_index("col")
@@ -37,8 +36,8 @@
     core = lax.rem(e, 2)
     up = lax.rem(band + 1, 4)
     down = lax.rem(band + 3, 4)
-    right = lax.rem(me + 1, NL)
-    left = lax.rem(me + NL - 1, NL)
+    right = z * NE + lax.rem(e + 1, NE)
+    left = z * NE + lax.rem(e + NE - 1, NE)
 
     barrier = pltpu.get_barrier_semaphore()
 
@@ -107,11 +106,12 @@
     def columns(owner):
         return pl.ds(pl.multiple_of(owner * 256, 256), 256)
 
+    planes = [lax.rem(z + step + NZ, NZ) for step in OFFSETS]
+
     def send_block(k, i):
         half = lax.div(k, NX)
-        there = lax.rem(z + offset(lax.div(i, 2)) + NZ, NZ)
-        place = lax.rem(x + lax.rem(k, NX), NX) * 2 + lax.rem(core + lax.rem(i, 2), 2)
-        to = there * NE + place
+        place = lax.rem(x + lax.rem(k, NX), NX) * 2 + (core if i % 2 == 0 else 1 - core)
+        to = planes[i // 2] * NE + place
         pltpu.make_async_remote_copy(
             src_ref=x_ref.at[:, half, :, columns(to)],
             dst_ref=field.at[half, z, e, :, :, pl.ds(TS, 2 * TS)],
@@ -121,6 +121,27 @@
             device_id_type=MESH,
         ).start()
 
+    def tile_ends(k, i, side):
+        half = lax.div(k, NX)
+        owner = planes[i] * NE + ENDS[side]
+        beyond = lax.rem(owner * 2 + (2 if side == 0 else 127), 128)
+        return (
+            x_ref.at[:, half, :, pl.ds(pl.multiple_of(beyond * TS, TS), TS)],
+            field.at[half, z, e, :, :, pl.ds(3 * TS if side == 0 else 0, TS)],
+            e_recv.at[half, x, side],
+        )
+
+    def send_tile(k, i, side):
+        source, target, arrived = tile_ends(k, i, side)
+        pltpu.make_async_remote_copy(
+            src_ref=source,
+            dst_ref=target,
+            send_sem=t_send.at[lax.div(k, NX), side],
+            recv_sem=arrived,
+            device_id={"lev": planes[i] * NE + ENDS[side]},
+            device_id_type=MESH,
+        ).start()
+
     def keep_block(half):
         pltpu.make_async_copy(
             x_ref.at[:, half, :, columns(me)],
@@ -128,18 +149,36 @@
             x_recv.at[half, x],
         ).start()
 
-    def send_round(k, first=0):
-        def one(i, carry):
+    def send_round(k):
+        for i in range(1, 2 * NZ):
             send_block(k, i)
-            return carry
-
-        lax.fori_loop(first, 2 * NZ, one, 0)
-
-    send_round(0, 1)
+
+        @pl.when(lax.rem(k, NX) != 0)
+        def _():
+            send_block(k, 0)
+
+        for side in range(2):
+            @pl.when(lax.rem(x + k, NX) == (NX - 1 if side == 0 else 0))
+            def _():
+                for i in range(1, NZ):
+                    send_tile(k, i, side)
+
+                @pl.when(e != ENDS[side])
+                def _():
+                    send_tile(k, 0, side)
+
+                @pl.when(e == ENDS[side])
+                def _():
+                    source, target, arrived = tile_ends(k, 0, side)
+                    pltpu.make_async_copy(source, target, arrived).start()
+
+    def first_rounds(k, carry):
+        send_round(k)
+        return carry
+
+    lax.fori_loop(0, WINDOW, first_rounds, 0)
     keep_block(0)
     keep_block(1)
-    for k in range(1, WINDOW):
-        send_round(k)
 
 
     local[3].wait()
@@ -200,31 +239,30 @@
                 jnp.bfloat16
             )
 
-            def send_back(i, inner):
-                there = lax.rem(z + offset(lax.div(i, 2)) + NZ, NZ)
-                spot = place * 2 + lax.rem(core + lax.rem(i, 2), 2)
-                to = there * NE + spot
-
-                @pl.when(to != me)
-                def _():
-                    pltpu.make_async_remote_copy(
-                        src_ref=result.at[half, there, spot],
-                        dst_ref=out_ref.at[:, half, :, columns(me)],
-                        send_sem=b_send,
-                        recv_sem=b_recv,
-                        device_id={"lev": to},
-                        device_id_type=MESH,
-                    ).start()
-
-                @pl.when(to == me)
-                def _():
-                    pltpu.make_async_copy(
-                        result.at[half, z, e], out_ref.at[:, half, :, columns(me)], b_recv
-                    ).start()
-
-                return inner
-
-            lax.fori_loop(0, 2 * NZ, send_back, 0)
+            def send_back(i):
+                spot = place * 2 + (core if i % 2 == 0 else 1 - core)
+                to = planes[i // 2] * NE + spot
+                pltpu.make_async_remote_copy(
+                    src_ref=result.at[half, planes[i // 2], spot],
+                    dst_ref=out_ref.at[:, half, :, columns(me)],
+                    send_sem=b_send,
+                    recv_sem=b_recv,
+                    device_id={"lev": to},
+                    device_id_type=MESH,
+                ).start()
+
+            for i in range(1, 2 * NZ):
+                send_back(i)
+
+            @pl.when(r != 0)
+            def _():
+                send_back(0)
+
+            @pl.when(r == 0)
+            def _():
+                pltpu.make_async_copy(
+                    result.at[half, z, e], out_ref.at[:, half, :, columns(me)], b_recv
+                ).start()
             return carry
 
         lax.fori_loop(0, NX, one_round, 0)
@@ -236,13 +274,18 @@
             g = group(lax.rem(k, NX))
             arrived = field.at[half, :, pl.ds(g * 2, 2), :, :, pl.ds(TS, 2 * TS)]
             pltpu.make_async_copy(arrived, arrived, x_recv.at[half, g]).wait()
-            edge(half, g, 0).start()
-            edge(half, g, 1).start()
+
+            @pl.when(e != 0)
+            def _():
+                edge(half, g, 0).start()
+
+            @pl.when(e != NE - 1)
+            def _():
+                edge(half, g, 1).start()
 
         @pl.when(k < ROUNDS - WINDOW)
         def _():
-            later = k + WINDOW
-            send_round(later, jnp.where(later == NX, 1, 0))
+            send_round(k + WINDOW)
 
         @pl.when(k == LAG_EDGE)
         def _():
@@ -254,8 +297,8 @@
             now = k - LAG_EDGE
             half = lax.div(now, NX)
             g = group(lax.rem(now + 1, NX))
-            edge(half, g, 0).wait()
-            edge(half, g, 1).wait()
+            edge(half, g, 0).wait_recv()
+            edge(half, g, 1).wait_recv()
             rows = field[half, :, pl.ds(g * 2, 2)].reshape(256, 4 * TS)
             for side in range(2):
                 part_out[side, half, g] = lax.dot_general(
@@ -296,6 +339,21 @@
         else:
             block = field.at[0, :, pl.ds(0, 2), :, :, pl.ds(TS, 2 * TS)]
             pltpu.make_async_copy(block, block, x_send.at[k]).wait()
+    for half in range(2):
+        for side in range(2):
+            block = field.at[half, pl.ds(0, NZ - 1), 0, :, :, pl.ds(0, TS)]
+            pltpu.make_async_copy(block, block, t_send.at[half, side]).wait()
+
+            @pl.when(e != ENDS[side])
+            def _():
+                block = field.at[half, 0, 0, :, :, pl.ds(0, TS)]
+                pltpu.make_async_copy(block, block, t_send.at[half, side]).wait()
+
+            @pl.when(e != (0 if side == 0 else NE - 1))
+            def _():
+                for g in range(NX):
+                    edge(half, g, side).wait_send()
+
     block = out_ref.at[:, :, :, pl.ds(0, (NL - 1) * 256)]
     pltpu.make_async_copy(block, block, b_send).wait()
     pltpu.make_async_copy(out_ref, out_ref, b_recv).wait()
@@ -337,6 +395,7 @@
             dma((2, NX)),
             dma((2, 2)),
             dma((2, 2)),
+            dma((2, 2)),
             dma((2, NX, 2)),
             dma((2, NX, 2)),
             dma((2, NX, 2)),

time: 73.8 us -> 71.7 us (0.972)
  Pallas kernels: 72.7 us -> 70.7 us
    pallas_call x1, Pallas kernels: 72.7 us -> 70.7 us  [body(): pl.pallas_call(kernel, out_shape=jax.ShapeDtypeStruct((2, 2, 8, NL * 256)...]
where the time goes in v4:
time: 71.7 us; the launch traced here: 71.6 us
  Pallas kernels  70.7 us (99%)
  local copies, waits for them, and re-layouts  0.97 us (1%)
    pallas_call x1, Pallas kernels, body(): pl.pallas_call(kernel, out_shape=jax.ShapeDtypeStruct((2, 2, 8, NL * 256)...  70.7 us

profile of v4, /device:TPU:1, one launch (start us, length us, event | category | flops | bytes accessed | tf_op | source)
XLA Modules:
  0.0 71.6 jit_solution(16705073650143392697)
XLA Ops:
  0.0 70.7 %shard_map.55 = bf16[2,2,8,16384]{3,2,1,0:T(8,128)(2,1)S(1)} custom-call(bf16[2,2,8,16384]{3,2,1,0:T(8,128)(2,1)} %bitcast.7, bf16[128,128]{1,0:T(8,128)(2,1)} %v_ref.1, bf16[2,9,128,128]{3,2,1,0:T(8,128)(2,1)} %bitcast.8, s32[2,9]{1,0:T(2,128)} %bitcast.9, s32[1,2]{1,0:T(1,128)} %count_hbm.1), custom_call_target="tpu_custom_call" | custom-call | tf_op jit(solution)/shard_map/pallas_call | solution.py:374
  70.7 1.0 %copy.8 = bf16[2,16,1,16384]{3,1,2,0:T(8,128)(2,1)} copy(bf16[2,16,1,16384]{3,1,2,0:T(8,128)(2,1)S(1)} %bitcast.6) | data formatting | bytes 2097152

commit v5 on v4

--- a/solution.py
+++ b/solution.py
@@ -18,7 +18,7 @@
 LAG_SUM = 4
 
 
-OFFSETS = (0, 1, -1, 2, -2, 3, -3, 4)
+OFFSETS = (0, 4, 3, -3, 2, -2, 1, -1)
 
 
 def kernel(
@@ -150,7 +150,7 @@
         ).start()
 
     def send_round(k):
-        for i in range(1, 2 * NZ):
+        for i in (*range(2, 2 * NZ), 1):
             send_block(k, i)
 
         @pl.when(lax.rem(k, NX) != 0)
@@ -230,7 +230,7 @@
 
     def answer(half):
         def one_round(r, carry):
-            place = lax.rem(x + r, NX)
+            place = lax.rem(x + r + 1, NX)
             rows = kron[:, place].reshape(256, 1024)
             block = jnp.dot(
                 rows, mixed[half].reshape(1024, 256), preferred_element_type=jnp.float32
@@ -251,14 +251,14 @@
                     device_id_type=MESH,
                 ).start()
 
-            for i in range(1, 2 * NZ):
+            for i in (*range(2, 2 * NZ), 1):
                 send_back(i)
 
-            @pl.when(r != 0)
+            @pl.when(r != NX - 1)
             def _():
                 send_back(0)
 
-            @pl.when(r == 0)
+            @pl.when(r == NX - 1)
             def _():
                 pltpu.make_async_copy(
                     result.at[half, z, e], out_ref.at[:, half, :, columns(me)], b_recv

time: 71.7 us -> 69.9 us (0.975)
  Pallas kernels: 70.7 us -> 68.8 us
    pallas_call x1, Pallas kernels: 70.7 us -> 68.8 us  [body(): pl.pallas_call(kernel, out_shape=jax.ShapeDtypeStruct((2, 2, 8, NL * 256)...]
where the time goes in v5:
time: 69.9 us; the launch traced here: 69.8 us
  Pallas kernels  68.8 us (98%)
  local copies, waits for them, and re-layouts  0.97 us (1%)
    pallas_call x1, Pallas kernels, body(): pl.pallas_call(kernel, out_shape=jax.ShapeDtypeStruct((2, 2, 8, NL * 256)...  68.8 us

profile of v5, /device:TPU:1, one launch (start us, length us, event | category | flops | bytes accessed | tf_op | source)
XLA Modules:
  0.0 69.8 jit_solution(336028811610390651)
XLA Ops:
  0.0 68.8 %shard_map.55 = bf16[2,2,8,16384]{3,2,1,0:T(8,128)(2,1)S(1)} custom-call(bf16[2,2,8,16384]{3,2,1,0:T(8,128)(2,1)} %bitcast.7, bf16[128,128]{1,0:T(8,128)(2,1)} %v_ref.1, bf16[2,9,128,128]{3,2,1,0:T(8,128)(2,1)} %bitcast.8, s32[2,9]{1,0:T(2,128)} %bitcast.9, s32[1,2]{1,0:T(1,128)} %count_hbm.1), custom_call_target="tpu_custom_call" | custom-call | tf_op jit(solution)/shard_map/pallas_call | solution.py:374
  68.8 1.0 %copy.8 = bf16[2,16,1,16384]{3,1,2,0:T(8,128)(2,1)} copy(bf16[2,16,1,16384]{3,1,2,0:T(8,128)(2,1)S(1)} %bitcast.6) | data formatting | bytes 2097152

commit v6 on v5

--- a/solution.py
+++ b/solution.py
@@ -13,7 +13,7 @@
 TS = 128
 ENDS = (NE - 1, 0)
 ROUNDS = 2 * NX
-WINDOW = 3
+WINDOW = 4
 LAG_EDGE = 2
 LAG_SUM = 4
 

time: 69.9 us -> 69.8 us (level)
  no operation moved by 1% of the time
where the time goes in v6:
time: 69.8 us; the launch traced here: 69.7 us
  Pallas kernels  68.7 us (98%)
  local copies, waits for them, and re-layouts  0.97 us (1%)
    pallas_call x1, Pallas kernels, body(): pl.pallas_call(kernel, out_shape=jax.ShapeDtypeStruct((2, 2, 8, NL * 256)...  68.7 us

profile of v6, /device:TPU:1, one launch (start us, length us, event | category | flops | bytes accessed | tf_op | source)
XLA Modules:
  0.0 69.7 jit_solution(14284125328586193363)
XLA Ops:
  0.0 68.7 %shard_map.55 = bf16[2,2,8,16384]{3,2,1,0:T(8,128)(2,1)S(1)} custom-call(bf16[2,2,8,16384]{3,2,1,0:T(8,128)(2,1)} %bitcast.7, bf16[128,128]{1,0:T(8,128)(2,1)} %v_ref.1, bf16[2,9,128,128]{3,2,1,0:T(8,128)(2,1)} %bitcast.8, s32[2,9]{1,0:T(2,128)} %bitcast.9, s32[1,2]{1,0:T(1,128)} %count_hbm.1), custom_call_target="tpu_custom_call" | custom-call | tf_op jit(solution)/shard_map/pallas_call | solution.py:374
  68.7 1.0 %copy.8 = bf16[2,16,1,16384]{3,1,2,0:T(8,128)(2,1)} copy(bf16[2,16,1,16384]{3,1,2,0:T(8,128)(2,1)S(1)} %bitcast.6) | data formatting | bytes 2097152
